TPU v7x, 1024 devices: a whole 4x8x16 slice. The times are simulated.
1024 devices in a mesh: blk: 16 (over y_hi, x, core), uly: 4 (over y_lo), batch: 16 (over z).
Axes of the slice: x: 4, y: 8 (y_hi: 2, y_lo: 4; y = y_hi * 4 + y_lo), z: 16, core: 2. Of those that a mesh axis runs over, the one named last changes fastest.
Arguments:
- queries: bfloat16 [131072, 1024], P(('batch', 'blk', 'uly')), parts along dimension 0, may hold values from -10 to 10
- keys: bfloat16 [131072, 1024], P(('batch', 'blk', 'uly')), parts along dimension 0, may hold values from -10 to 10
- values: bfloat16 [131072, 1024], P(('batch', 'blk', 'uly')), parts along dimension 0, may hold values from -6 to 6
- out_grad: bfloat16 [131072, 1024], P(('batch', 'blk', 'uly')), parts along dimension 0, may hold values from -16 to 16
- block_mask: int32 [1024, 64], P('batch'), parts along dimension 0, may hold values from 0 to 1, as said below
Outputs:
- query_grad: bfloat16 [131072, 1024], P(('batch', 'blk', 'uly')), parts along dimension 0
- key_grad: bfloat16 [131072, 1024], P(('batch', 'blk', 'uly')), parts along dimension 0
- value_grad: bfloat16 [131072, 1024], P(('batch', 'blk', 'uly')), parts along dimension 0
There are 16 independent parts, one for each index of `batch`. A program takes and returns all parts, laid end to end along the dimension named above; each array names one. Nothing has to cross between parts.
Inputs may be any that keep to these rules, and one draw needn't show every extreme that they name: block_mask[a, b] is 1 for every two blocks a, b of the same cell (cell c holds tokens c * 512 to (c + 1) * 512 - 1); for blocks of different cells it is 1 only where the two cells are neighbours on the closed chain of 16 cells (cell c beside cells c - 1 and c + 1 modulo 16), and 0 for all other pairs.
All inputs are finite; a program needn't handle non-finite values.
Results may differ from a plain program's by a relative error of at most 0.0096.
Values may be sent and summed in bfloat16 or wider, within the bound.
A program may use at most 32 MiB of HBM per device.

v0:
```python
import math

import jax
import jax.numpy as jnp
from jax import lax
from jax.sharding import PartitionSpec as P

HEAD_DIM = 128


def padded(block, sides, width):
    for axis, dim in sides:
        count = lax.axis_size(axis)
        forward = [(i, i + 1) for i in range(count - 1)]
        forward.append((count - 1, 0))
        backward = [(target, source) for source, target in forward]
        low = lax.ppermute(
            lax.slice_in_dim(block, block.shape[dim] - width, None, axis=dim), axis, forward
        )
        high = lax.ppermute(lax.slice_in_dim(block, 0, width, axis=dim), axis, backward)
        block = jnp.concatenate([low, block, high], axis=dim)
    return block


def passed_along(block, axis, distance):
    devices = range(lax.axis_size(axis))
    route = [((i - distance) % len(devices), i) for i in devices]
    return lax.ppermute(block, axis, route)


def times_t(left, right):
    return lax.dot_general(
        left, right, (((1,), (1,)), ((), ())), preferred_element_type=jnp.float32
    )


def t_times(left, right):
    return lax.dot_general(
        left, right, (((0,), (0,)), ((), ())), preferred_element_type=jnp.float32
    )


def widen_blocks(mask_blocks):
    return jnp.repeat(jnp.repeat(mask_blocks > 0, 128, axis=0), 128, axis=1)


def local(queries, keys, values, out_grad, block_mask):
    local_q, local_k, local_v, local_g = (
        lax.all_to_all(queries, "uly", split_axis=1, concat_axis=0, tiled=True),
        lax.all_to_all(keys, "uly", split_axis=1, concat_axis=0, tiled=True),
        lax.all_to_all(values, "uly", split_axis=1, concat_axis=0, tiled=True),
        lax.all_to_all(out_grad, "uly", split_axis=1, concat_axis=0, tiled=True),
    )
    genes = local_q.shape[0]
    heads_here = local_q.shape[1] // HEAD_DIM
    scale = 1.0 / math.sqrt(HEAD_DIM)
    cells = lax.axis_size("blk")
    here = lax.axis_index("blk")
    per_cell = genes // 128
    near = (here + jnp.array([-1, 0, 1], dtype=jnp.int32) + cells) % cells
    mask_rows = lax.dynamic_slice_in_dim(block_mask, here * per_cell, per_cell, 0).reshape(
        per_cell, cells, per_cell
    )
    row_mask = widen_blocks(jnp.take(mask_rows, near, axis=1).reshape(per_cell, 3 * per_cell))
    pairs = jnp.stack([local_k, local_v], axis=1)
    band = padded(pairs, (("blk", 0),), genes)
    q_grads = []
    k_parts = []
    v_parts = []
    for head in range(heads_here):
        lower = head * HEAD_DIM
        upper = lower + HEAD_DIM
        q_head = local_q[:, lower:upper]
        g_head = local_g[:, lower:upper]
        k_band = band[:, 0, lower:upper]
        v_band = band[:, 1, lower:upper]
        scores = jnp.where(row_mask, times_t(q_head, k_band) * scale, -1e30)
        top = jnp.max(scores, axis=1, keepdims=True)
        total = jnp.sum(jnp.where(row_mask, jnp.exp(scores - top), 0.0), axis=1, keepdims=True)
        lse = top + jnp.log(total)
        probs = jnp.where(row_mask, jnp.exp(scores - lse), 0.0)
        dprobs = times_t(g_head, v_band)
        delta = jnp.sum(probs * dprobs, axis=1, keepdims=True)
        dscores = (probs * (dprobs - delta)).astype(jnp.bfloat16)
        q_grads.append(
            (jnp.dot(dscores, k_band, preferred_element_type=jnp.float32) * scale).astype(
                jnp.bfloat16
            )
        )
        k_parts.append(t_times(dscores, q_head))
        v_parts.append(t_times(probs.astype(jnp.bfloat16), g_head))
    query_grad = jnp.concatenate(q_grads, axis=1)
    partial_terms = jnp.stack(
        [jnp.concatenate(k_parts, axis=1), jnp.concatenate(v_parts, axis=1)], axis=1
    )
    from_next = passed_along(partial_terms[:genes].astype(jnp.bfloat16), "blk", -1).astype(
        jnp.float32
    )
    from_prior = passed_along(partial_terms[2 * genes :].astype(jnp.bfloat16), "blk", 1).astype(
        jnp.float32
    )
    summed = partial_terms[genes : 2 * genes] + from_next + from_prior
    key_grad = (summed[:, 0] * scale).astype(jnp.bfloat16)
    value_grad = summed[:, 1].astype(jnp.bfloat16)
    return (
        lax.all_to_all(query_grad, "uly", split_axis=0, concat_axis=1, tiled=True),
        lax.all_to_all(key_grad, "uly", split_axis=0, concat_axis=1, tiled=True),
        lax.all_to_all(value_grad, "uly", split_axis=0, concat_axis=1, tiled=True),
    )


def solution(mesh):
    return jax.shard_map(
        local,
        mesh=mesh,
        in_specs=(
            P(("batch", "blk", "uly"), None),
            P(("batch", "blk", "uly"), None),
            P(("batch", "blk", "uly"), None),
            P(("batch", "blk", "uly"), None),
            P("batch", None),
        ),
        out_specs=(
            P(("batch", "blk", "uly"), None),
            P(("batch", "blk", "uly"), None),
            P(("batch", "blk", "uly"), None),
        ),
        check_vma=False,
    )
```

profile of v0, /device:TPU:8, one launch (start us, length us, event | category | flops | bytes accessed | tf_op | source)
XLA Modules:
  0.0 133.5 jit_solution(5871558233368867670)
XLA Ops:
  0.6 0.0 copy-start
  0.7 1.8 %copy.36 = bf16[128,1024]{0,1:T(8,128)(2,1)} copy(bf16[128,1024]{1,0:T(8,128)(2,1)} %param.7) | data formatting | bytes 524288 | tf_op args[1]
  2.5 16.5 %all-to-all-start = ((bf16[128,4,256]{0,2,1:T(8,128)(2,1)}), bf16[128,4,256]{0,2,1:T(8,128)(2,1)S(1)}, u32[]{:S(2)}, u32[]{:S(2)}) async-start(bf16[128,4,256]{0,2,1:T(8,128)(2,1)} %bitcast.2), calls=%async_computation | async-start | bytes 524288 | tf_op jit(solution)/shard_map/all_to_all | solution.py:50
  19.0 1.8 %copy.38 = bf16[128,1024]{0,1:T(8,128)(2,1)} copy(bf16[128,1024]{1,0:T(8,128)(2,1)} %param.8) | data formatting | bytes 524288 | tf_op args[2]
  20.8 4.4 %all-to-all-done = bf16[128,4,256]{0,2,1:T(8,128)(2,1)S(1)} async-done(((bf16[128,4,256]{0,2,1:T(8,128)(2,1)}), bf16[128,4,256]{0,2,1:T(8,128)(2,1)S(1)}, u32[]{:S(2)}, u32[]{:S(2)}) %all-to-all-start) | async-done | bytes 262176 | tf_op jit(solution)/shard_map/all_to_all | solution.py:50
  25.2 4.0 %all-to-all-start.1 = ((bf16[128,4,256]{0,2,1:T(8,128)(2,1)}), bf16[128,4,256]{0,2,1:T(8,128)(2,1)S(1)}, u32[]{:S(2)}, u32[]{:S(2)}) async-start(bf16[128,4,256]{0,2,1:T(8,128)(2,1)} %bitcast.5), calls=%async_computation.1 | async-start | bytes 524288 | tf_op jit(solution)/shard_map/all_to_all | solution.py:51
  29.2 1.8 %copy.40 = bf16[128,1024]{0,1:T(8,128)(2,1)} copy(bf16[128,1024]{1,0:T(8,128)(2,1)} %param.6) | data formatting | bytes 524288 | tf_op args[0]
  31.0 4.4 %all-to-all-done.1 = bf16[128,4,256]{0,2,1:T(8,128)(2,1)S(1)} async-done(((bf16[128,4,256]{0,2,1:T(8,128)(2,1)}), bf16[128,4,256]{0,2,1:T(8,128)(2,1)S(1)}, u32[]{:S(2)}, u32[]{:S(2)}) %all-to-all-start.1) | async-done | bytes 262176 | tf_op jit(solution)/shard_map/all_to_all | solution.py:51
  35.4 4.0 %all-to-all-start.2 = ((bf16[128,4,256]{0,2,1:T(8,128)(2,1)}), bf16[128,4,256]{0,2,1:T(8,128)(2,1)S(1)}, u32[]{:S(2)}, u32[]{:S(2)}) async-start(bf16[128,4,256]{0,2,1:T(8,128)(2,1)} %bitcast.9), calls=%async_computation.2 | async-start | bytes 524288 | tf_op jit(solution)/shard_map/all_to_all | solution.py:49
  39.4 0.1 broadcast_in_dim.39
  39.5 0.1 broadcast_in_dim.40
  39.6 0.1 reshape.72
  39.7 0.1 copy.37
  39.9 0.1 copy.39
  40.0 0.1 pad_maximum_fusion.2
  40.1 1.9 %collective-permute-start.1 = (bf16[512,2,256]{2,0,1:T(8,128)(2,1)S(1)}, bf16[512,2,256]{2,0,1:T(8,128)(2,1)S(1)}, u32[]{:S(2)}, u32[]{:S(2)}) collective-permute-start(bf16[512,2,256]{2,0,1:T(8,128)(2,1)S(1)} %pad_maximum_fusion.2), channel_id=1, source_target_pairs={{64,0},{128,64},{192,128},{256,192},{320,256},{384,320},{448,384},... | collective-permute-start | bytes 1572872 | tf_op jit(solution)/shard_map/ppermute | solution.py:20
  42.0 2.4 %collective-permute-start = (bf16[512,2,256]{2,0,1:T(8,128)(2,1)S(1)}, bf16[512,2,256]{2,0,1:T(8,128)(2,1)S(1)}, u32[]{:S(2)}, u32[]{:S(2)}) collective-permute-start(bf16[512,2,256]{2,0,1:T(8,128)(2,1)S(1)} %pad_maximum_fusion.2), channel_id=1, source_target_pairs={{0,64},{64,128},{128,192},{192,256},{256,320},{320,384},{384,448},... | collective-permute-start | bytes 1572872 | tf_op jit(solution)/shard_map/ppermute | solution.py:17
  44.4 0.6 gather_fusion
  45.0 0.1 gather.7
  45.1 0.8 copy.42
  45.9 11.1 %all-to-all-done.2 = bf16[128,4,256]{0,2,1:T(8,128)(2,1)S(1)} async-done(((bf16[128,4,256]{0,2,1:T(8,128)(2,1)}), bf16[128,4,256]{0,2,1:T(8,128)(2,1)S(1)}, u32[]{:S(2)}, u32[]{:S(2)}) %all-to-all-start.2) | async-done | bytes 262176 | tf_op jit(solution)/shard_map/all_to_all | solution.py:49
  57.0 6.0 %all-to-all-start.3 = ((bf16[128,4,256]{0,2,1:T(8,128)(2,1)}), bf16[128,4,256]{0,2,1:T(8,128)(2,1)S(1)}, u32[]{:S(2)}, u32[]{:S(2)}) async-start(bf16[128,4,256]{0,2,1:T(8,128)(2,1)} %bitcast.14), calls=%async_computation.3 | async-start | bytes 524288 | tf_op jit(solution)/shard_map/all_to_all | solution.py:52
  63.0 0.1 copy.35
  63.2 0.1 broadcast_bitcast_fusion
  63.3 0.1 copy.41
  63.4 5.8 %all-to-all-done.3 = bf16[128,4,256]{0,2,1:T(8,128)(2,1)S(1)} async-done(((bf16[128,4,256]{0,2,1:T(8,128)(2,1)}), bf16[128,4,256]{0,2,1:T(8,128)(2,1)S(1)}, u32[]{:S(2)}, u32[]{:S(2)}) %all-to-all-start.3) | async-done | bytes 262176 | tf_op jit(solution)/shard_map/all_to_all | solution.py:52
  69.2 0.1 copy.43
  69.4 0.1 pad_maximum_fusion.1
  69.5 0.6 fusion.28
  70.1 0.6 fusion.27
  70.7 0.6 convolution_bitcast_fusion
  71.3 1.1 fusion.3
  72.4 1.4 %multiply_reduce_fusion.1 = (f32[512]{0:T(512)S(1)}, f32[512]{0:T(512)S(1)}, f32[512,1536]{0,1:T(8,128)S(1)}) fusion(f32[512,1536]{0,1:T(8,128)S(1)} %get-tuple-element.21, f32[512]{0:T(512)S(1)} %get-tuple-element.26, pred[512,12]{0,1:T(8,128)(4,1)S(1)} %bitcast.124, f32[512,1536]{0,1:T(8,128)S(1)} %convolution_bitcast_fusion, ...), kind=kOutput, calls=%fused_computation.22 | convolution fusion | flops 207617024 | bytes 13123584 | tf_op jit(solution)/shard_map/dot_general | solution.py:32
  73.8 2.1 %fusion.5 = (bf16[512,1536]{0,1:T(8,128)(2,1)S(1)}, bf16[512,1536]{0,1:T(8,128)(2,1)S(1)}, bf16[512,1536]{0,1:T(8,128)(2,1)S(1)}, bf16[512,1536]{0,1:T(8,128)(2,1)S(1)}) fusion(f32[512,1536]{0,1:T(8,128)S(1)} %get-tuple-element.21, f32[512]{0:T(512)S(1)} %get-tuple-element.26, pred[512,12]{0,1:T(8,128)(4,1)S(1)} %bitcast.125, ...), kind=kLoop, calls=%fused_computation.23 | loop fusion | flops 9437184 | bytes 18888704 | tf_op jit(solution)/shard_map/convert_element_type | solution.py:91
  75.8 0.7 fusion.19
  76.5 0.7 fusion.13
  77.1 0.7 fusion.16
  77.8 0.7 fusion.22
  78.5 0.1 maximum_bitcast_fusion.1
  78.6 0.1 maximum_bitcast_fusion
  78.7 0.2 fusion.2
  78.9 1.0 fusion.26
  80.0 1.9 %collective-permute-start.2 = (bf16[512,2,256]{0,2,1:T(8,128)(2,1)}, bf16[512,2,256]{0,2,1:T(8,128)(2,1)}, u32[]{:S(2)}, u32[]{:S(2)}) collective-permute-start(bf16[512,2,256]{0,2,1:T(8,128)(2,1)} %get-tuple-element.16), channel_id=1, source_target_pairs={{64,0},{128,64},{192,128},{256,192},{320,256},{384,320},{448,384},... | collective-permute-start | bytes 1572872 | tf_op jit(solution)/shard_map/ppermute | solution.py:28
  81.9 2.4 %collective-permute-start.3 = (bf16[512,2,256]{0,2,1:T(8,128)(2,1)}, bf16[512,2,256]{0,2,1:T(8,128)(2,1)}, u32[]{:S(2)}, u32[]{:S(2)}) collective-permute-start(bf16[512,2,256]{0,2,1:T(8,128)(2,1)} %get-tuple-element.17), channel_id=1, source_target_pairs={{960,0},{0,64},{64,128},{128,192},{192,256},{256,320},{320,384},{3... | collective-permute-start | bytes 1572872 | tf_op jit(solution)/shard_map/ppermute | solution.py:28
  84.3 0.4 fusion.7
  84.7 0.4 fusion.8
  85.2 0.7 copy_bitcast_fusion
  85.9 4.0 %all-to-all-start.4 = ((bf16[4,128,256]{1,2,0:T(8,128)(2,1)}), bf16[4,128,256]{1,2,0:T(8,128)(2,1)S(1)}, u32[]{:S(2)}, u32[]{:S(2)}) async-start(bf16[4,128,256]{1,2,0:T(8,128)(2,1)} %copy_bitcast_fusion), calls=%async_computation.4 | async-start | bytes 524288 | tf_op jit(solution)/shard_map/all_to_all | solution.py:106
  89.9 6.7 %collective-permute-done.2 = bf16[512,2,256]{0,2,1:T(8,128)(2,1)} collective-permute-done((bf16[512,2,256]{0,2,1:T(8,128)(2,1)}, bf16[512,2,256]{0,2,1:T(8,128)(2,1)}, u32[]{:S(2)}, u32[]{:S(2)}) %collective-permute-start.2) | collective-permute-done | bytes 524320 | tf_op jit(solution)/shard_map/ppermute | solution.py:28
  96.6 10.1 %collective-permute-done.3 = bf16[512,2,256]{0,2,1:T(8,128)(2,1)} collective-permute-done((bf16[512,2,256]{0,2,1:T(8,128)(2,1)}, bf16[512,2,256]{0,2,1:T(8,128)(2,1)}, u32[]{:S(2)}, u32[]{:S(2)}) %collective-permute-start.3) | collective-permute-done | bytes 524320 | tf_op jit(solution)/shard_map/ppermute | solution.py:28
  106.7 1.4 %fusion.11 = f32[512,2,256]{0,2,1:T(8,128)S(1)} fusion(f32[1536,1,256]{0,2,1:T(8,128)S(1)} %maximum_bitcast_fusion, f32[1536,1,256]{0,2,1:T(8,128)S(1)} %maximum_bitcast_fusion.1, bf16[512,2,256]{0,2,1:T(8,128)(2,1)} %collective-permute-done.3, bf16[512,2,256]{0,2,1:T(8,128)(2,1)} %collective-permute-done.2), kind=kLoop, calls=%fused_computation.34 | loop fusion | flops 1310720 | bytes 5242880 | tf_op jit(solution)/shard_map/add | solution.py:102
  108.1 1.0 copy-done.1
  109.1 0.1 convert_element_type.48
  109.2 0.7 copy.46
  109.9 3.4 %all-to-all-start.6 = ((bf16[4,128,256]{1,2,0:T(8,128)(2,1)}), bf16[4,128,256]{1,2,0:T(8,128)(2,1)S(1)}, u32[]{:S(2)}, u32[]{:S(2)}) async-start(bf16[4,128,256]{1,2,0:T(8,128)(2,1)} %copy.46), calls=%async_computation.6 | async-start | bytes 524288 | tf_op jit(solution)/shard_map/all_to_all | solution.py:108
  113.3 1.1 fusion.12
  114.4 0.1 convert_element_type.47
  114.5 0.7 copy.45
  115.2 6.0 %all-to-all-done.6 = bf16[4,128,256]{1,2,0:T(8,128)(2,1)S(1)} async-done(((bf16[4,128,256]{1,2,0:T(8,128)(2,1)}), bf16[4,128,256]{1,2,0:T(8,128)(2,1)S(1)}, u32[]{:S(2)}, u32[]{:S(2)}) %all-to-all-start.6) | async-done | bytes 262176 | tf_op jit(solution)/shard_map/all_to_all | solution.py:108
  121.2 5.2 %all-to-all-start.5 = ((bf16[4,128,256]{1,2,0:T(8,128)(2,1)}), bf16[4,128,256]{1,2,0:T(8,128)(2,1)S(1)}, u32[]{:S(2)}, u32[]{:S(2)}) async-start(bf16[4,128,256]{1,2,0:T(8,128)(2,1)} %copy.45), calls=%async_computation.5 | async-start | bytes 524288 | tf_op jit(solution)/shard_map/all_to_all | solution.py:107
  126.4 0.8 copy.47
  127.2 0.8 copy.49
  128.1 4.5 %all-to-all-done.5 = bf16[4,128,256]{1,2,0:T(8,128)(2,1)S(1)} async-done(((bf16[4,128,256]{1,2,0:T(8,128)(2,1)}), bf16[4,128,256]{1,2,0:T(8,128)(2,1)S(1)}, u32[]{:S(2)}, u32[]{:S(2)}) %all-to-all-start.5) | async-done | bytes 262176 | tf_op jit(solution)/shard_map/all_to_all | solution.py:107
  132.6 0.8 copy.48
  (19 shorter events, 0.1 us)
Async XLA Ops:
  0.6 39.0 %copy-start = (s32[64,64]{1,0:T(8,128)S(1)}, s32[64,64]{1,0:T(8,128)}, u32[]{:S(2)}) copy-start(s32[64,64]{1,0:T(8,128)} %param.10) | copy-start | bytes 49156
  0.6 38.8 %copy-start.3 = (s32[3]{0:T(128)S(1)}, s32[3]{0:T(128)}, u32[]{:S(2)}) copy-start(s32[3]{0:T(128)} %constant.53.clone) | copy-start | bytes 40
  0.7 44.4 %copy-start.2 = (bf16[128,1024]{1,0:T(8,128)(2,1)S(1)}, bf16[128,1024]{1,0:T(8,128)(2,1)}, u32[]{:S(2)}) copy-start(bf16[128,1024]{1,0:T(8,128)(2,1)} %param.9) | copy-start | bytes 786436
  2.5 22.7 %all-to-all-start = ((bf16[128,4,256]{0,2,1:T(8,128)(2,1)}), bf16[128,4,256]{0,2,1:T(8,128)(2,1)S(1)}, u32[]{:S(2)}, u32[]{:S(2)}) async-start(bf16[128,4,256]{0,2,1:T(8,128)(2,1)} %bitcast.2), calls=%async_computation | async-start | bytes 524288 | tf_op jit(solution)/shard_map/all_to_all | solution.py:50
  25.2 10.2 %all-to-all-start.1 = ((bf16[128,4,256]{0,2,1:T(8,128)(2,1)}), bf16[128,4,256]{0,2,1:T(8,128)(2,1)S(1)}, u32[]{:S(2)}, u32[]{:S(2)}) async-start(bf16[128,4,256]{0,2,1:T(8,128)(2,1)} %bitcast.5), calls=%async_computation.1 | async-start | bytes 524288 | tf_op jit(solution)/shard_map/all_to_all | solution.py:51
  35.4 21.6 %all-to-all-start.2 = ((bf16[128,4,256]{0,2,1:T(8,128)(2,1)}), bf16[128,4,256]{0,2,1:T(8,128)(2,1)S(1)}, u32[]{:S(2)}, u32[]{:S(2)}) async-start(bf16[128,4,256]{0,2,1:T(8,128)(2,1)} %bitcast.9), calls=%async_computation.2 | async-start | bytes 524288 | tf_op jit(solution)/shard_map/all_to_all | solution.py:49
  40.1 29.3 %collective-permute-start.1 = (bf16[512,2,256]{2,0,1:T(8,128)(2,1)S(1)}, bf16[512,2,256]{2,0,1:T(8,128)(2,1)S(1)}, u32[]{:S(2)}, u32[]{:S(2)}) collective-permute-start(bf16[512,2,256]{2,0,1:T(8,128)(2,1)S(1)} %pad_maximum_fusion.2), channel_id=1, source_target_pairs={{64,0},{128,64},{192,128},{256,192},{320,256},{384,320},{448,384},... | collective-permute-start | bytes 1572872 | tf_op jit(solution)/shard_map/ppermute | solution.py:20
  42.0 27.4 %collective-permute-start = (bf16[512,2,256]{2,0,1:T(8,128)(2,1)S(1)}, bf16[512,2,256]{2,0,1:T(8,128)(2,1)S(1)}, u32[]{:S(2)}, u32[]{:S(2)}) collective-permute-start(bf16[512,2,256]{2,0,1:T(8,128)(2,1)S(1)} %pad_maximum_fusion.2), channel_id=1, source_target_pairs={{0,64},{64,128},{128,192},{192,256},{256,320},{320,384},{384,448},... | collective-permute-start | bytes 1572872 | tf_op jit(solution)/shard_map/ppermute | solution.py:17
  57.0 12.2 %all-to-all-start.3 = ((bf16[128,4,256]{0,2,1:T(8,128)(2,1)}), bf16[128,4,256]{0,2,1:T(8,128)(2,1)S(1)}, u32[]{:S(2)}, u32[]{:S(2)}) async-start(bf16[128,4,256]{0,2,1:T(8,128)(2,1)} %bitcast.14), calls=%async_computation.3 | async-start | bytes 524288 | tf_op jit(solution)/shard_map/all_to_all | solution.py:52
  80.0 16.6 %collective-permute-start.2 = (bf16[512,2,256]{0,2,1:T(8,128)(2,1)}, bf16[512,2,256]{0,2,1:T(8,128)(2,1)}, u32[]{:S(2)}, u32[]{:S(2)}) collective-permute-start(bf16[512,2,256]{0,2,1:T(8,128)(2,1)} %get-tuple-element.16), channel_id=1, source_target_pairs={{64,0},{128,64},{192,128},{256,192},{320,256},{384,320},{448,384},... | collective-permute-start | bytes 1572872 | tf_op jit(solution)/shard_map/ppermute | solution.py:28
  81.9 24.8 %collective-permute-start.3 = (bf16[512,2,256]{0,2,1:T(8,128)(2,1)}, bf16[512,2,256]{0,2,1:T(8,128)(2,1)}, u32[]{:S(2)}, u32[]{:S(2)}) collective-permute-start(bf16[512,2,256]{0,2,1:T(8,128)(2,1)} %get-tuple-element.17), channel_id=1, source_target_pairs={{960,0},{0,64},{64,128},{128,192},{192,256},{256,320},{320,384},{3... | collective-permute-start | bytes 1572872 | tf_op jit(solution)/shard_map/ppermute | solution.py:28
  85.9 24.0 %all-to-all-start.4 = ((bf16[4,128,256]{1,2,0:T(8,128)(2,1)}), bf16[4,128,256]{1,2,0:T(8,128)(2,1)S(1)}, u32[]{:S(2)}, u32[]{:S(2)}) async-start(bf16[4,128,256]{1,2,0:T(8,128)(2,1)} %copy_bitcast_fusion), calls=%async_computation.4 | async-start | bytes 524288 | tf_op jit(solution)/shard_map/all_to_all | solution.py:106
  108.1 1.0 copy-start.1
  109.9 11.3 %all-to-all-start.6 = ((bf16[4,128,256]{1,2,0:T(8,128)(2,1)}), bf16[4,128,256]{1,2,0:T(8,128)(2,1)S(1)}, u32[]{:S(2)}, u32[]{:S(2)}) async-start(bf16[4,128,256]{1,2,0:T(8,128)(2,1)} %copy.46), calls=%async_computation.6 | async-start | bytes 524288 | tf_op jit(solution)/shard_map/all_to_all | solution.py:108
  121.2 11.4 %all-to-all-start.5 = ((bf16[4,128,256]{1,2,0:T(8,128)(2,1)}), bf16[4,128,256]{1,2,0:T(8,128)(2,1)S(1)}, u32[]{:S(2)}, u32[]{:S(2)}) async-start(bf16[4,128,256]{1,2,0:T(8,128)(2,1)} %copy.45), calls=%async_computation.5 | async-start | bytes 524288 | tf_op jit(solution)/shard_map/all_to_all | solution.py:107
where the time goes:
time: 134 us; the launch traced here: 133 us
  waiting for transfers between devices  53 us (40%)
  starting transfers between devices  51.7 us (39%)
  local copies, waits for them, and re-layouts  14.2 us (11%)
  other arithmetic  7.01 us (5%)
  matrix products  6.61 us (5%)
    ppermute x2, waiting for transfers between devices, passed_along(): return lax.ppermute(block, axis, route)  16.8 us
    all_to_all x1, starting transfers between devices, local(): lax.all_to_all(keys, 'uly', split_axis=1, concat_axis=0, tiled=True)  16.5 us
    all_to_all x1, waiting for transfers between devices, local(): lax.all_to_all(queries, 'uly', split_axis=1, concat_axis=0, tiled=True)  11.1 us
    unnamed x18, local copies, waits for them, and re-layouts  9.89 us
    all_to_all x1, starting transfers between devices, local(): lax.all_to_all(out_grad, 'uly', split_axis=1, concat_axis=0, tiled=True)  6 us
    all_to_all x1, waiting for transfers between devices, local(): lax.all_to_all(value_grad, 'uly', split_axis=0, concat_axis=1, tiled=True)  5.97 us
    all_to_all x1, waiting for transfers between devices, local(): lax.all_to_all(out_grad, 'uly', split_axis=1, concat_axis=0, tiled=True)  5.82 us
    all_to_all x1, starting transfers between devices, local(): lax.all_to_all(key_grad, 'uly', split_axis=0, concat_axis=1, tiled=True)  5.19 us
  transfers between devices with their start and end apart: 11, of which 8 were waited for; matrix products, arithmetic and copies ran while one was open for 10% of the time, Pallas kernels for 0%

commit v1 on v0

v1 whole, which is shorter than its diff:
```python
import functools
import math

import jax
import jax.numpy as jnp
from jax import lax
from jax.experimental import pallas as pl
from jax.experimental.pallas import tpu as pltpu
from jax.sharding import PartitionSpec as P

MESH = pl.DeviceIdType.MESH
DIM = 128
BLOCK = 128
HEADS_HERE = 2
F32 = jnp.float32
BF16 = jnp.bfloat16


def times_t(left, right):
    return lax.dot_general(left, right, (((1,), (1,)), ((), ())), preferred_element_type=F32)


def groups_sum(block):
    rows, columns = block.shape
    return jnp.sum(block.reshape(rows // 8, 8, columns), axis=0)


def groups_max(block):
    rows, columns = block.shape
    return jnp.max(block.reshape(rows // 8, 8, columns), axis=0)


def kernel(
    cells,
    ulys,
    q_hbm,
    k_hbm,
    v_hbm,
    g_hbm,
    mask_hbm,
    dq_hbm,
    dk_hbm,
    dv_hbm,
    kv,
    qg,
    scores,
    dprobs,
    probs_low,
    dscores,
    own,
    sides,
    landed,
    results,
    mask,
    mask_sem,
    local_sem,
    in_send,
    in_recv,
    band_send,
    band_recv,
    part_send,
    part_recv,
    out_local,
    out_send,
    out_recv,
):
    b = lax.axis_index("blk")
    u = lax.axis_index("uly")
    rows = q_hbm.shape[0]
    genes = rows * ulys
    per_cell = genes // BLOCK
    half = cells // 2

    def group_of(blk, uly):
        upper = blk // half
        return uly + upper * (ulys - 1 - 2 * uly)

    prior = lax.rem(b + cells - 1, cells)
    following = lax.rem(b + 1, cells)
    my_group = group_of(b, u)
    prior_uly = group_of(prior, my_group)
    following_uly = group_of(following, my_group)
    sideways = (
        {"blk": prior, "uly": prior_uly},
        {"blk": following, "uly": following_uly},
    )

    def peer(step):
        return lax.rem(u + step, ulys)

    barrier = pltpu.get_barrier_semaphore()
    for step in range(1, ulys):
        pl.semaphore_signal(
            barrier, inc=1, device_id={"uly": peer(step)}, device_id_type=MESH
        )
    for side in sideways:
        pl.semaphore_signal(barrier, inc=1, device_id=side, device_id_type=MESH)

    mask_rows = (b * per_cell // 8) * 8
    mask_copy = pltpu.make_async_copy(
        mask_hbm.at[pl.ds(pl.multiple_of(mask_rows, 8), 8), :], mask, mask_sem
    )
    mask_copy.start()

    sources = (k_hbm, v_hbm, q_hbm, g_hbm)

    def landing(head, which, uly):
        at = pl.ds(pl.multiple_of(uly * rows, rows), rows)
        if which < 2:
            return kv.at[head, which, 1, at, :]
        return qg.at[head, which - 2, at, :]

    def columns_of(group, head):
        start = (group * HEADS_HERE + head) * DIM
        return pl.ds(pl.multiple_of(start, DIM), DIM)

    def entry_local(head, which):
        return pltpu.make_async_copy(
            sources[which].at[:, columns_of(my_group, head)],
            landing(head, which, u),
            local_sem.at[head, which],
        )

    def entry_copy(head, which, step):
        to = peer(step)
        return pltpu.make_async_remote_copy(
            src_ref=sources[which].at[:, columns_of(group_of(b, to), head)],
            dst_ref=landing(head, which, u),
            send_sem=in_send.at[head, which, step - 1],
            recv_sem=in_recv.at[head, which, step - 1],
            device_id={"uly": to},
            device_id_type=MESH,
        )

    def entry_arrival(head, which, step):
        came_from = lax.rem(u + ulys - step, ulys)
        return pltpu.make_async_remote_copy(
            src_ref=sources[which].at[:, columns_of(my_group, head)],
            dst_ref=landing(head, which, came_from),
            send_sem=in_send.at[head, which, step - 1],
            recv_sem=in_recv.at[head, which, step - 1],
            device_id={"uly": came_from},
            device_id_type=MESH,
        )

    for head in range(HEADS_HERE):
        for which in range(4):
            entry_local(head, which).start()

    pl.semaphore_wait(barrier, ulys + 1)

    for head in range(HEADS_HERE):
        for which in range(4):
            for step in range(1, ulys):
                entry_copy(head, which, step).start()

    def await_entry(head, which):
        entry_local(head, which).wait()
        for step in range(1, ulys):
            entry_arrival(head, which, step).wait_recv()

    def band_copy(head, which, side):
        return pltpu.make_async_remote_copy(
            src_ref=kv.at[head, which, 1],
            dst_ref=kv.at[head, which, 2 - 2 * side],
            send_sem=band_send.at[head, which, side],
            recv_sem=band_recv.at[head, which, side],
            device_id=sideways[side],
            device_id_type=MESH,
        )

    def band_arrival(head, which, side):
        return pltpu.make_async_remote_copy(
            src_ref=kv.at[head, which, 1],
            dst_ref=kv.at[head, which, 2 - 2 * side],
            send_sem=band_send.at[head, which, side],
            recv_sem=band_recv.at[head, which, side],
            device_id=sideways[side],
            device_id_type=MESH,
        )

    def send_band(head):
        for which in range(2):
            await_entry(head, which)
            for side in range(2):
                band_copy(head, which, side).start()

    def part_copy(head, which, side):
        return pltpu.make_async_remote_copy(
            src_ref=sides.at[head, which, side],
            dst_ref=landed.at[head, which, 1 - side],
            send_sem=part_send.at[head, which, side],
            recv_sem=part_recv.at[head, which, side],
            device_id=sideways[side],
            device_id_type=MESH,
        )

    outs = (dq_hbm, dk_hbm, dv_hbm)

    def exit_local(head, which):
        return pltpu.make_async_copy(
            results.at[head, which, pl.ds(pl.multiple_of(u * rows, rows), rows), :],
            outs[which].at[:, columns_of(my_group, head)],
            out_local.at[head, which],
        )

    def exit_copy(head, which, step):
        to = peer(step)
        return pltpu.make_async_remote_copy(
            src_ref=results.at[head, which, pl.ds(pl.multiple_of(to * rows, rows), rows), :],
            dst_ref=outs[which].at[:, columns_of(my_group, head)],
            send_sem=out_send.at[head, which, step - 1],
            recv_sem=out_recv.at[head, which, step - 1],
            device_id={"uly": to},
            device_id_type=MESH,
        )

    def exit_arrival(head, which, step):
        came_from = lax.rem(u + ulys - step, ulys)
        return pltpu.make_async_remote_copy(
            src_ref=results.at[head, which, pl.ds(0, rows), :],
            dst_ref=outs[which].at[:, columns_of(group_of(b, came_from), head)],
            send_sem=out_send.at[head, which, step - 1],
            recv_sem=out_recv.at[head, which, step - 1],
            device_id={"uly": came_from},
            device_id_type=MESH,
        )

    def send_out(head, which):
        exit_local(head, which).start()
        for step in range(1, ulys):
            exit_copy(head, which, step).start()

    scale = 1.0 / math.sqrt(DIM)
    scale2 = scale * math.log2(math.e)
    first_row = lax.rem(b * per_cell, 8)
    near = (prior, b, following)

    def bias_row(part, block):
        pieces = []
        for a in range(per_cell):
            allowed = mask[first_row + a, near[part] * per_cell + block] > 0
            pieces.append(jnp.full((1, BLOCK), jnp.where(allowed, 0.0, -1e30), F32))
        return jnp.concatenate(pieces, axis=1)

    parts = [(part, block) for part in range(3) for block in range(per_cell)]

    def compute(head):
        q = qg[head, 0]
        g = qg[head, 1]
        top = None
        for part, block in parts:
            at = slice(block * BLOCK, (block + 1) * BLOCK)
            s = times_t(kv[head, 0, part, at, :], q) * scale2 + bias_row(part, block)
            scores[part, at, :] = s
            here = groups_max(s)
            top = here if top is None else jnp.maximum(top, here)
            dprobs[part, at, :] = times_t(kv[head, 1, part, at, :], g)
        top = jnp.max(top, axis=0, keepdims=True)
        total = jnp.zeros((8, genes), F32)
        delta = jnp.zeros((8, genes), F32)
        for part, block in parts:
            at = slice(block * BLOCK, (block + 1) * BLOCK)
            e = jnp.exp2(scores[part, at, :] - top)
            scores[part, at, :] = e
            total += groups_sum(e)
            delta += groups_sum(e * dprobs[part, at, :])
        inverse = 1.0 / jnp.sum(total, axis=0, keepdims=True)
        delta = jnp.sum(delta, axis=0, keepdims=True) * inverse
        for part, block in parts:
            at = slice(block * BLOCK, (block + 1) * BLOCK)
            p = scores[part, at, :] * inverse
            probs_low[part, at, :] = p.astype(BF16)
            dscores[part, at, :] = (p * (dprobs[part, at, :] - delta)).astype(BF16)
        for side in range(2):
            sides[head, 0, side] = jnp.dot(
                dscores[2 * side], q, preferred_element_type=F32
            ).astype(BF16)
            part_copy(head, 0, side).start()
            sides[head, 1, side] = jnp.dot(
                probs_low[2 * side], g, preferred_element_type=F32
            ).astype(BF16)
            part_copy(head, 1, side).start()
        grad = jnp.zeros((DIM, genes), F32)
        for part in range(3):
            grad += jnp.dot(kv[head, 0, part].T, dscores[part], preferred_element_type=F32)
        results[head, 0] = (grad.T * scale).astype(BF16)
        send_out(head, 0)
        own[head, 0] = jnp.dot(dscores[1], q, preferred_element_type=F32)
        own[head, 1] = jnp.dot(probs_low[1], g, preferred_element_type=F32)

    def finish(head):
        for which, factor in ((0, scale), (1, None)):
            for side in range(2):
                part_copy(head, which, side).wait_recv()
            summed = (
                own[head, which]
                + landed[head, which, 1].astype(F32)
                + landed[head, which, 0].astype(F32)
            )
            if factor is not None:
                summed = summed * factor
            results[head, 1 + which] = summed.astype(BF16)
            send_out(head, 1 + which)

    def await_rest(head):
        for which in range(2, 4):
            await_entry(head, which)
        for which in range(2):
            for side in range(2):
                band_arrival(head, which, side).wait_recv()

    send_band(0)
    mask_copy.wait()
    await_rest(0)
    send_band(1)
    compute(0)
    await_rest(1)
    finish(0)
    compute(1)
    finish(1)

    for head in range(HEADS_HERE):
        for which in range(4):
            for step in range(1, ulys):
                entry_copy(head, which, step).wait_send()
        for which in range(2):
            for side in range(2):
                band_copy(head, which, side).wait_send()
                part_copy(head, which, side).wait_send()
        for which in range(3):
            exit_local(head, which).wait()
            for step in range(1, ulys):
                exit_copy(head, which, step).wait_send()
                exit_arrival(head, which, step).wait_recv()


def local(cells, ulys, queries, keys, values, out_grad, block_mask):
    rows, width = queries.shape
    genes = rows * ulys
    n = HEADS_HERE
    dma = pltpu.SemaphoreType.DMA
    outputs = [jax.ShapeDtypeStruct((rows, width), BF16)] * 3
    return pl.pallas_call(
        functools.partial(kernel, cells, ulys),
        out_shape=outputs,
        in_specs=[pl.BlockSpec(memory_space=pl.ANY)] * 5,
        out_specs=[pl.BlockSpec(memory_space=pl.ANY)] * 3,
        scratch_shapes=[
            pltpu.VMEM((n, 2, 3, genes, DIM), BF16),
            pltpu.VMEM((n, 2, genes, DIM), BF16),
            pltpu.VMEM((3, genes, genes), F32),
            pltpu.VMEM((3, genes, genes), F32),
            pltpu.VMEM((3, genes, genes), BF16),
            pltpu.VMEM((3, genes, genes), BF16),
            pltpu.VMEM((n, 2, genes, DIM), F32),
            pltpu.VMEM((n, 2, 2, genes, DIM), BF16),
            pltpu.VMEM((n, 2, 2, genes, DIM), BF16),
            pltpu.VMEM((n, 3, genes, DIM), BF16),
            pltpu.SMEM((8, block_mask.shape[1]), jnp.int32),
            dma,
            dma((n, 4)),
            dma((n, 4, ulys - 1)),
            dma((n, 4, ulys - 1)),
            dma((n, 2, 2)),
            dma((n, 2, 2)),
            dma((n, 2, 2)),
            dma((n, 2, 2)),
            dma((n, 3)),
            dma((n, 3, ulys - 1)),
            dma((n, 3, ulys - 1)),
        ],
        compiler_params=pltpu.CompilerParams(
            collective_id=0, has_side_effects=True, vmem_limit_bytes=48 * 1024 * 1024
        ),
    )(queries, keys, values, out_grad, block_mask)


def solution(mesh):
    rows = P(("batch", "blk", "uly"), None)
    return jax.shard_map(
        functools.partial(local, mesh.shape["blk"], mesh.shape["uly"]),
        mesh=mesh,
        in_specs=(rows, rows, rows, rows, P("batch", None)),
        out_specs=(rows, rows, rows),
        check_vma=False,
    )
```

time: 134 us -> 69.7 us (0.52)
  the two profiles are of different devices: /device:TPU:8 before, /device:TPU:63 now
where the time goes in v1:
time: 69.7 us; the launch traced here: 69.4 us
  Pallas kernels  62 us (89%)
  local copies, waits for them, and re-layouts  6.66 us (10%)
    pallas_call x1, Pallas kernels, local(): pl.pallas_call(functools.partial(kernel, cells, ulys), out_shape=outputs,...  62 us
    unnamed x13, local copies, waits for them, and re-layouts  6.66 us

profile of v1, /device:TPU:63, one launch (start us, length us, event | category | flops | bytes accessed | tf_op | source)
XLA Modules:
  0.0 69.4 jit_solution(14862803520546402051)
XLA Ops:
  0.6 0.0 copy-start
  0.6 0.9 %copy-done = bf16[128,1024]{1,0:T(8,128)(2,1)S(1)} copy-done((bf16[128,1024]{1,0:T(8,128)(2,1)S(1)}, bf16[128,1024]{1,0:T(8,128)(2,1)}, u32[]{:S(2)}) %copy-start) | copy-done | bytes 262168
  1.6 0.0 copy-start.1
  1.6 0.9 %copy-done.1 = bf16[128,1024]{1,0:T(8,128)(2,1)S(1)} copy-done((bf16[128,1024]{1,0:T(8,128)(2,1)S(1)}, bf16[128,1024]{1,0:T(8,128)(2,1)}, u32[]{:S(2)}) %copy-start.1) | copy-done | bytes 262168
  2.5 0.0 copy-start.2
  2.5 0.9 %copy-done.2 = bf16[128,1024]{1,0:T(8,128)(2,1)S(1)} copy-done((bf16[128,1024]{1,0:T(8,128)(2,1)S(1)}, bf16[128,1024]{1,0:T(8,128)(2,1)}, u32[]{:S(2)}) %copy-start.2) | copy-done | bytes 262168
  3.5 0.0 copy-start.3
  3.5 0.9 %copy-done.3 = bf16[128,1024]{1,0:T(8,128)(2,1)S(1)} copy-done((bf16[128,1024]{1,0:T(8,128)(2,1)S(1)}, bf16[128,1024]{1,0:T(8,128)(2,1)}, u32[]{:S(2)}) %copy-start.3) | copy-done | bytes 262168
  4.4 0.0 copy-start.4
  4.4 0.8 %copy-done.4 = s32[64,64]{1,0:T(8,128)S(1)} copy-done((s32[64,64]{1,0:T(8,128)S(1)}, s32[64,64]{1,0:T(8,128)}, u32[]{:S(2)}) %copy-start.4) | copy-done | bytes 16408
  5.2 62.0 %shard_map.76 = (bf16[128,1024]{1,0:T(8,128)(2,1)S(1)}, bf16[128,1024]{1,0:T(8,128)(2,1)S(1)}, bf16[128,1024]{1,0:T(8,128)(2,1)S(1)}) custom-call(bf16[128,1024]{1,0:T(8,128)(2,1)S(1)} %copy-done, bf16[128,1024]{1,0:T(8,128)(2,1)S(1)} %copy-done.1, bf16[128,1024]{1,0:T(8,128)(2,1)S(1)} %copy-done.2, bf16[128,1024]{1,0:T(8,128)(2,1)S(1)} %copy-done.3, ...), custom_call_target="tpu_custom_call" | custom-call | tf_op jit(solution)/shard_map/pallas_call | solution.py:344
  67.2 0.7 %copy.11 = bf16[128,1024]{1,0:T(8,128)(2,1)} copy(bf16[128,1024]{1,0:T(8,128)(2,1)S(1)} %get-tuple-element.6) | data formatting | bytes 524288
  67.9 0.7 %copy.12 = bf16[128,1024]{1,0:T(8,128)(2,1)} copy(bf16[128,1024]{1,0:T(8,128)(2,1)S(1)} %get-tuple-element.7) | data formatting | bytes 524288
  68.7 0.7 %copy.13 = bf16[128,1024]{1,0:T(8,128)(2,1)} copy(bf16[128,1024]{1,0:T(8,128)(2,1)S(1)} %get-tuple-element.8) | data formatting | bytes 524288
Async XLA Ops:
  0.6 1.0 %copy-start = (bf16[128,1024]{1,0:T(8,128)(2,1)S(1)}, bf16[128,1024]{1,0:T(8,128)(2,1)}, u32[]{:S(2)}) copy-start(bf16[128,1024]{1,0:T(8,128)(2,1)} %q_hbm.1) | copy-start | bytes 786436
  1.6 0.9 %copy-start.1 = (bf16[128,1024]{1,0:T(8,128)(2,1)S(1)}, bf16[128,1024]{1,0:T(8,128)(2,1)}, u32[]{:S(2)}) copy-start(bf16[128,1024]{1,0:T(8,128)(2,1)} %k_hbm.1) | copy-start | bytes 786436
  2.5 0.9 %copy-start.2 = (bf16[128,1024]{1,0:T(8,128)(2,1)S(1)}, bf16[128,1024]{1,0:T(8,128)(2,1)}, u32[]{:S(2)}) copy-start(bf16[128,1024]{1,0:T(8,128)(2,1)} %v_hbm.1) | copy-start | bytes 786436
  3.5 0.9 %copy-start.3 = (bf16[128,1024]{1,0:T(8,128)(2,1)S(1)}, bf16[128,1024]{1,0:T(8,128)(2,1)}, u32[]{:S(2)}) copy-start(bf16[128,1024]{1,0:T(8,128)(2,1)} %g_hbm.1) | copy-start | bytes 786436
  4.4 0.8 %copy-start.4 = (s32[64,64]{1,0:T(8,128)S(1)}, s32[64,64]{1,0:T(8,128)}, u32[]{:S(2)}) copy-start(s32[64,64]{1,0:T(8,128)} %mask_hbm.1) | copy-start | bytes 49156

commit v2 on v1

--- a/solution.py
+++ b/solution.py
@@ -143,16 +143,17 @@
             device_id_type=MESH,
         )
 
-    for head in range(HEADS_HERE):
-        for which in range(4):
+    for which in range(4):
+        for head in range(HEADS_HERE):
             entry_local(head, which).start()
 
     pl.semaphore_wait(barrier, ulys + 1)
 
-    for head in range(HEADS_HERE):
-        for which in range(4):
-            for step in range(1, ulys):
-                entry_copy(head, which, step).start()
+    for pair in ((0, 1), (2, 3)):
+        for head in range(HEADS_HERE):
+            for which in pair:
+                for step in range(1, ulys):
+                    entry_copy(head, which, step).start()
 
     def await_entry(head, which):
         entry_local(head, which).wait()
@@ -285,7 +286,6 @@
         for part in range(3):
             grad += jnp.dot(kv[head, 0, part].T, dscores[part], preferred_element_type=F32)
         results[head, 0] = (grad.T * scale).astype(BF16)
-        send_out(head, 0)
         own[head, 0] = jnp.dot(dscores[1], q, preferred_element_type=F32)
         own[head, 1] = jnp.dot(probs_low[1], g, preferred_element_type=F32)
 
@@ -310,14 +310,16 @@
             for side in range(2):
                 band_arrival(head, which, side).wait_recv()
 
+    mask_copy.wait()
     send_band(0)
-    mask_copy.wait()
+    send_band(1)
     await_rest(0)
-    send_band(1)
     compute(0)
     await_rest(1)
+    send_out(0, 0)
+    compute(1)
+    send_out(1, 0)
     finish(0)
-    compute(1)
     finish(1)
 
     for head in range(HEADS_HERE):
@@ -335,16 +337,25 @@
                 exit_arrival(head, which, step).wait_recv()
 
 
+def settle(dq, dk, dv, dq_out, dk_out, dv_out, sems):
+    pairs = ((dq, dq_out), (dk, dk_out), (dv, dv_out))
+    copies = [pltpu.make_async_copy(*pair, sems.at[i]) for i, pair in enumerate(pairs)]
+    for copy in copies:
+        copy.start()
+    for copy in copies:
+        copy.wait()
+
+
 def local(cells, ulys, queries, keys, values, out_grad, block_mask):
     rows, width = queries.shape
     genes = rows * ulys
     n = HEADS_HERE
     dma = pltpu.SemaphoreType.DMA
     outputs = [jax.ShapeDtypeStruct((rows, width), BF16)] * 3
-    return pl.pallas_call(
+    grads = pl.pallas_call(
         functools.partial(kernel, cells, ulys),
         out_shape=outputs,
-        in_specs=[pl.BlockSpec(memory_space=pl.ANY)] * 5,
+        in_specs=[pl.BlockSpec(memory_space=pltpu.HBM)] * 5,
         out_specs=[pl.BlockSpec(memory_space=pl.ANY)] * 3,
         scratch_shapes=[
             pltpu.VMEM((n, 2, 3, genes, DIM), BF16),
@@ -371,9 +382,17 @@
             dma((n, 3, ulys - 1)),
         ],
         compiler_params=pltpu.CompilerParams(
-            collective_id=0, has_side_effects=True, vmem_limit_bytes=48 * 1024 * 1024
+            collective_id=0, has_side_effects=True, vmem_limit_bytes=40 * 1024 * 1024
         ),
-    )(queries, keys, values, out_grad, block_mask)
+    )(*(pltpu.with_memory_space_constraint(x, pltpu.HBM) for x in (queries, keys, values, out_grad, block_mask)))
+    return pl.pallas_call(
+        settle,
+        out_shape=outputs,
+        in_specs=[pl.BlockSpec(memory_space=pl.ANY)] * 3,
+        out_specs=[pl.BlockSpec(memory_space=pltpu.HBM)] * 3,
+        scratch_shapes=[dma((3,))],
+        compiler_params=pltpu.CompilerParams(vmem_limit_bytes=1024 * 1024),
+    )(*grads)
 
 
 def solution(mesh):

time: 69.7 us -> 63.7 us (0.914)
  the two profiles are of different devices: /device:TPU:63 before, /device:TPU:1 now
where the time goes in v2:
time: 63.7 us; the launch traced here: 63.5 us
  Pallas kernels  62.9 us (99%)
  between operations  0.64 us (1%)
    pallas_call x1, Pallas kernels, local(): pl.pallas_call(functools.partial(kernel, cells, ulys), out_shape=outputs,...  62 us

profile of v2, /device:TPU:1, one launch (start us, length us, event | category | flops | bytes accessed | tf_op | source)
XLA Modules:
  0.0 63.5 jit_solution(3319074424294343913)
XLA Ops:
  0.6 62.0 %shard_map.76 = (bf16[128,1024]{1,0:T(8,128)(2,1)S(1)}, bf16[128,1024]{1,0:T(8,128)(2,1)S(1)}, bf16[128,1024]{1,0:T(8,128)(2,1)S(1)}) custom-call(bf16[128,1024]{1,0:T(8,128)(2,1)} %q_hbm.1, bf16[128,1024]{1,0:T(8,128)(2,1)} %k_hbm.1, bf16[128,1024]{1,0:T(8,128)(2,1)} %v_hbm.1, bf16[128,1024]{1,0:T(8,128)(2,1)} %g_hbm.1, s32[64,64]{1,0:T(8,128)} %mask_hbm.1), custom_call_target="tpu_custom_call" | custom-call | tf_op jit(solution)/shard_map/pallas_call | solution.py:355
  62.6 0.9 %shard_map.77 = (bf16[128,1024]{1,0:T(8,128)(2,1)}, bf16[128,1024]{1,0:T(8,128)(2,1)}, bf16[128,1024]{1,0:T(8,128)(2,1)}) custom-call(bf16[128,1024]{1,0:T(8,128)(2,1)S(1)} %get-tuple-element.6.dq, bf16[128,1024]{1,0:T(8,128)(2,1)S(1)} %get-tuple-element.7.dk, bf16[128,1024]{1,0:T(8,128)(2,1)S(1)} %get-tuple-element.8.dv), custom_call_target="tpu_custom_call" | custom-call | tf_op jit(solution)/shard_map/pallas_call | solution.py:388

commit v3 on v2

--- a/solution.py
+++ b/solution.py
@@ -53,6 +53,8 @@
     results,
     mask,
     mask_sem,
+    ready,
+    ready_side,
     local_sem,
     in_send,
     in_recv,
@@ -88,13 +90,19 @@
     def peer(step):
         return lax.rem(u + step, ulys)
 
+    listens = lax.rem(b + 1, 2)
     barrier = pltpu.get_barrier_semaphore()
     for step in range(1, ulys):
-        pl.semaphore_signal(
-            barrier, inc=1, device_id={"uly": peer(step)}, device_id_type=MESH
-        )
-    for side in sideways:
-        pl.semaphore_signal(barrier, inc=1, device_id=side, device_id_type=MESH)
+        to = peer(step)
+
+        @pl.when((to < u) | ((u == ulys - 2) & (to == ulys - 1)))
+        def _():
+            pl.semaphore_signal(barrier, inc=1, device_id={"uly": to}, device_id_type=MESH)
+
+    @pl.when(listens == 0)
+    def _():
+        for side in sideways:
+            pl.semaphore_signal(barrier, inc=1, device_id=side, device_id_type=MESH)
 
     mask_rows = (b * per_cell // 8) * 8
     mask_copy = pltpu.make_async_copy(
@@ -147,13 +155,43 @@
         for head in range(HEADS_HERE):
             entry_local(head, which).start()
 
-    pl.semaphore_wait(barrier, ulys + 1)
-
-    for pair in ((0, 1), (2, 3)):
+    pl.semaphore_wait(barrier, jnp.where(u == ulys - 1, 1, ulys - 1 - u) + 2 * listens)
+    for step in range(1, ulys):
+        to = peer(step)
+
+        @pl.when(to > u)
+        def _():
+            pl.semaphore_signal(
+                ready.at[step - 1], inc=1, device_id={"uly": to}, device_id_type=MESH
+            )
+
+    @pl.when(listens == 1)
+    def _():
+        for side in range(2):
+            pl.semaphore_signal(
+                ready_side.at[1 - side], inc=1, device_id=sideways[side], device_id_type=MESH
+            )
+
+    for last in (False, True):
+        for step in range(1, ulys):
+            to = peer(step)
+
+            @pl.when((to < u) & ((to == 0) == last))
+            def _():
+                pl.semaphore_wait(ready.at[ulys - 1 - step], 1)
+
         for head in range(HEADS_HERE):
-            for which in pair:
+            for which in range(2):
                 for step in range(1, ulys):
-                    entry_copy(head, which, step).start()
+
+                    @pl.when((peer(step) == 0) == last)
+                    def _():
+                        entry_copy(head, which, step).start()
+
+    for head in range(HEADS_HERE):
+        for which in range(2, 4):
+            for step in range(1, ulys):
+                entry_copy(head, which, step).start()
 
     def await_entry(head, which):
         entry_local(head, which).wait()
@@ -311,6 +349,12 @@
                 band_arrival(head, which, side).wait_recv()
 
     mask_copy.wait()
+
+    @pl.when(listens == 0)
+    def _():
+        for side in range(2):
+            pl.semaphore_wait(ready_side.at[side], 1)
+
     send_band(0)
     send_band(1)
     await_rest(0)
@@ -370,6 +414,8 @@
             pltpu.VMEM((n, 3, genes, DIM), BF16),
             pltpu.SMEM((8, block_mask.shape[1]), jnp.int32),
             dma,
+            pltpu.SemaphoreType.REGULAR((ulys - 1,)),
+            pltpu.SemaphoreType.REGULAR((2,)),
             dma((n, 4)),
             dma((n, 4, ulys - 1)),
             dma((n, 4, ulys - 1)),

time: 63.7 us -> 60.1 us (0.943)
  the two profiles are of different devices: /device:TPU:1 before, /device:TPU:24 now
where the time goes in v3:
time: 60.1 us; the launch traced here: 59.9 us
  Pallas kernels  59.3 us (99%)
  between operations  0.64 us (1%)
    pallas_call x1, Pallas kernels, local(): pl.pallas_call(functools.partial(kernel, cells, ulys), out_shape=outputs,...  58.4 us

profile of v3, /device:TPU:24, one launch (start us, length us, event | category | flops | bytes accessed | tf_op | source)
XLA Modules:
  0.0 59.9 jit_solution(2318045909047368962)
XLA Ops:
  0.6 58.4 %shard_map.76 = (bf16[128,1024]{1,0:T(8,128)(2,1)S(1)}, bf16[128,1024]{1,0:T(8,128)(2,1)S(1)}, bf16[128,1024]{1,0:T(8,128)(2,1)S(1)}) custom-call(bf16[128,1024]{1,0:T(8,128)(2,1)} %q_hbm.1, bf16[128,1024]{1,0:T(8,128)(2,1)} %k_hbm.1, bf16[128,1024]{1,0:T(8,128)(2,1)} %v_hbm.1, bf16[128,1024]{1,0:T(8,128)(2,1)} %g_hbm.1, s32[64,64]{1,0:T(8,128)} %mask_hbm.1), custom_call_target="tpu_custom_call" | custom-call | tf_op jit(solution)/shard_map/pallas_call | solution.py:399
  59.0 0.9 %shard_map.77 = (bf16[128,1024]{1,0:T(8,128)(2,1)}, bf16[128,1024]{1,0:T(8,128)(2,1)}, bf16[128,1024]{1,0:T(8,128)(2,1)}) custom-call(bf16[128,1024]{1,0:T(8,128)(2,1)S(1)} %get-tuple-element.6.dq, bf16[128,1024]{1,0:T(8,128)(2,1)S(1)} %get-tuple-element.7.dk, bf16[128,1024]{1,0:T(8,128)(2,1)S(1)} %get-tuple-element.8.dv), custom_call_target="tpu_custom_call" | custom-call | tf_op jit(solution)/shard_map/pallas_call | solution.py:434

commit v4 on v3

--- a/solution.py
+++ b/solution.py
@@ -188,7 +188,7 @@
                     def _():
                         entry_copy(head, which, step).start()
 
-    for head in range(HEADS_HERE):
+    def start_rest(head):
         for which in range(2, 4):
             for step in range(1, ulys):
                 entry_copy(head, which, step).start()
@@ -220,7 +220,6 @@
 
     def send_band(head):
         for which in range(2):
-            await_entry(head, which)
             for side in range(2):
                 band_copy(head, which, side).start()
 
@@ -284,51 +283,64 @@
 
     parts = [(part, block) for part in range(3) for block in range(per_cell)]
 
-    def compute(head):
+    def block_rows(block):
+        return slice(block * BLOCK, (block + 1) * BLOCK)
+
+    def softmax(head):
+        q = qg[head, 0]
+        top = None
+        for part, block in parts:
+            at = block_rows(block)
+            s = times_t(kv[head, 0, part, at, :], q) * scale2 + bias_row(part, block)
+            scores[head, part, at, :] = s
+            here = groups_max(s)
+            top = here if top is None else jnp.maximum(top, here)
+        top = jnp.max(top, axis=0, keepdims=True)
+        total = jnp.zeros((8, genes), F32)
+        for part, block in parts:
+            at = block_rows(block)
+            e = jnp.exp2(scores[head, part, at, :] - top)
+            scores[head, part, at, :] = e
+            total += groups_sum(e)
+        inverse = 1.0 / jnp.sum(total, axis=0, keepdims=True)
+        for part, block in parts:
+            at = block_rows(block)
+            probs_low[head, part, at, :] = (scores[head, part, at, :] * inverse).astype(BF16)
+        return inverse
+
+    def gradients(head, inverse):
         q = qg[head, 0]
         g = qg[head, 1]
-        top = None
-        for part, block in parts:
-            at = slice(block * BLOCK, (block + 1) * BLOCK)
-            s = times_t(kv[head, 0, part, at, :], q) * scale2 + bias_row(part, block)
-            scores[part, at, :] = s
-            here = groups_max(s)
-            top = here if top is None else jnp.maximum(top, here)
-            dprobs[part, at, :] = times_t(kv[head, 1, part, at, :], g)
-        top = jnp.max(top, axis=0, keepdims=True)
-        total = jnp.zeros((8, genes), F32)
+        for side in range(2):
+            sides[head, 1, side] = jnp.dot(
+                probs_low[head, 2 * side], g, preferred_element_type=F32
+            ).astype(BF16)
+            part_copy(head, 1, side).start()
         delta = jnp.zeros((8, genes), F32)
         for part, block in parts:
-            at = slice(block * BLOCK, (block + 1) * BLOCK)
-            e = jnp.exp2(scores[part, at, :] - top)
-            scores[part, at, :] = e
-            total += groups_sum(e)
-            delta += groups_sum(e * dprobs[part, at, :])
-        inverse = 1.0 / jnp.sum(total, axis=0, keepdims=True)
+            at = block_rows(block)
+            d = times_t(kv[head, 1, part, at, :], g)
+            dprobs[part, at, :] = d
+            delta += groups_sum(scores[head, part, at, :] * d)
         delta = jnp.sum(delta, axis=0, keepdims=True) * inverse
         for part, block in parts:
-            at = slice(block * BLOCK, (block + 1) * BLOCK)
-            p = scores[part, at, :] * inverse
-            probs_low[part, at, :] = p.astype(BF16)
+            at = block_rows(block)
+            p = scores[head, part, at, :] * inverse
             dscores[part, at, :] = (p * (dprobs[part, at, :] - delta)).astype(BF16)
         for side in range(2):
             sides[head, 0, side] = jnp.dot(
                 dscores[2 * side], q, preferred_element_type=F32
             ).astype(BF16)
             part_copy(head, 0, side).start()
-            sides[head, 1, side] = jnp.dot(
-                probs_low[2 * side], g, preferred_element_type=F32
-            ).astype(BF16)
-            part_copy(head, 1, side).start()
         grad = jnp.zeros((DIM, genes), F32)
         for part in range(3):
             grad += jnp.dot(kv[head, 0, part].T, dscores[part], preferred_element_type=F32)
         results[head, 0] = (grad.T * scale).astype(BF16)
+        own[head, 1] = jnp.dot(probs_low[head, 1], g, preferred_element_type=F32)
         own[head, 0] = jnp.dot(dscores[1], q, preferred_element_type=F32)
-        own[head, 1] = jnp.dot(probs_low[1], g, preferred_element_type=F32)
 
     def finish(head):
-        for which, factor in ((0, scale), (1, None)):
+        for which, factor in ((1, None), (0, scale)):
             for side in range(2):
                 part_copy(head, which, side).wait_recv()
             summed = (
@@ -341,14 +353,15 @@
             results[head, 1 + which] = summed.astype(BF16)
             send_out(head, 1 + which)
 
-    def await_rest(head):
-        for which in range(2, 4):
-            await_entry(head, which)
-        for which in range(2):
-            for side in range(2):
-                band_arrival(head, which, side).wait_recv()
+    def await_band(head, which):
+        for side in range(2):
+            band_arrival(head, which, side).wait_recv()
 
     mask_copy.wait()
+
+    for which in range(2):
+        await_entry(0, which)
+    start_rest(0)
 
     @pl.when(listens == 0)
     def _():
@@ -356,12 +369,23 @@
             pl.semaphore_wait(ready_side.at[side], 1)
 
     send_band(0)
+    for which in range(2):
+        await_entry(1, which)
+    start_rest(1)
     send_band(1)
-    await_rest(0)
-    compute(0)
-    await_rest(1)
+    await_entry(0, 2)
+    await_band(0, 0)
+    inverse = softmax(0)
+    await_entry(0, 3)
+    await_band(0, 1)
+    gradients(0, inverse)
+    await_entry(1, 2)
+    await_band(1, 0)
+    inverse = softmax(1)
+    await_entry(1, 3)
     send_out(0, 0)
-    compute(1)
+    await_band(1, 1)
+    gradients(1, inverse)
     send_out(1, 0)
     finish(0)
     finish(1)
@@ -404,9 +428,9 @@
         scratch_shapes=[
             pltpu.VMEM((n, 2, 3, genes, DIM), BF16),
             pltpu.VMEM((n, 2, genes, DIM), BF16),
+            pltpu.VMEM((n, 3, genes, genes), F32),
             pltpu.VMEM((3, genes, genes), F32),
-            pltpu.VMEM((3, genes, genes), F32),
-            pltpu.VMEM((3, genes, genes), BF16),
+            pltpu.VMEM((n, 3, genes, genes), BF16),
             pltpu.VMEM((3, genes, genes), BF16),
             pltpu.VMEM((n, 2, genes, DIM), F32),
             pltpu.VMEM((n, 2, 2, genes, DIM), BF16),

time: 60.1 us -> 56.2 us (0.935)
  Pallas kernels: 59.3 us -> 55.3 us
    pallas_call x1, Pallas kernels: 58.4 us -> 54.4 us  [local(): pl.pallas_call(functools.partial(kernel, cells, ulys), out_shape=outputs,...]
where the time goes in v4:
time: 56.2 us; the launch traced here: 55.9 us
  Pallas kernels  55.3 us (98%)
  between operations  0.64 us (1%)
    pallas_call x1, Pallas kernels, local(): pl.pallas_call(functools.partial(kernel, cells, ulys), out_shape=outputs,...  54.4 us

profile of v4, /device:TPU:24, one launch (start us, length us, event | category | flops | bytes accessed | tf_op | source)
XLA Modules:
  0.0 55.9 jit_solution(3379388207419867644)
XLA Ops:
  0.6 54.4 %shard_map.76 = (bf16[128,1024]{1,0:T(8,128)(2,1)S(1)}, bf16[128,1024]{1,0:T(8,128)(2,1)S(1)}, bf16[128,1024]{1,0:T(8,128)(2,1)S(1)}) custom-call(bf16[128,1024]{1,0:T(8,128)(2,1)} %q_hbm.1, bf16[128,1024]{1,0:T(8,128)(2,1)} %k_hbm.1, bf16[128,1024]{1,0:T(8,128)(2,1)} %v_hbm.1, bf16[128,1024]{1,0:T(8,128)(2,1)} %g_hbm.1, s32[64,64]{1,0:T(8,128)} %mask_hbm.1), custom_call_target="tpu_custom_call" | custom-call | tf_op jit(solution)/shard_map/pallas_call | solution.py:423
  55.0 0.9 %shard_map.77 = (bf16[128,1024]{1,0:T(8,128)(2,1)}, bf16[128,1024]{1,0:T(8,128)(2,1)}, bf16[128,1024]{1,0:T(8,128)(2,1)}) custom-call(bf16[128,1024]{1,0:T(8,128)(2,1)S(1)} %get-tuple-element.6.dq, bf16[128,1024]{1,0:T(8,128)(2,1)S(1)} %get-tuple-element.7.dk, bf16[128,1024]{1,0:T(8,128)(2,1)S(1)} %get-tuple-element.8.dv), custom_call_target="tpu_custom_call" | custom-call | tf_op jit(solution)/shard_map/pallas_call | solution.py:458

commit v5 on v4

--- a/solution.py
+++ b/solution.py
@@ -386,8 +386,8 @@
     send_out(0, 0)
     await_band(1, 1)
     gradients(1, inverse)
+    finish(0)
     send_out(1, 0)
-    finish(0)
     finish(1)
 
     for head in range(HEADS_HERE):

time: 56.2 us -> 55.2 us (0.982)
  the two profiles are of different devices: /device:TPU:24 before, /device:TPU:56 now
where the time goes in v5:
time: 55.2 us; the launch traced here: 55 us
  Pallas kernels  54.4 us (99%)
  between operations  0.64 us (1%)
    pallas_call x1, Pallas kernels, local(): pl.pallas_call(functools.partial(kernel, cells, ulys), out_shape=outputs,...  53.4 us

profile of v5, /device:TPU:56, one launch (start us, length us, event | category | flops | bytes accessed | tf_op | source)
XLA Modules:
  0.0 55.0 jit_solution(16519848949607398882)
XLA Ops:
  0.6 53.4 %shard_map.76 = (bf16[128,1024]{1,0:T(8,128)(2,1)S(1)}, bf16[128,1024]{1,0:T(8,128)(2,1)S(1)}, bf16[128,1024]{1,0:T(8,128)(2,1)S(1)}) custom-call(bf16[128,1024]{1,0:T(8,128)(2,1)} %q_hbm.1, bf16[128,1024]{1,0:T(8,128)(2,1)} %k_hbm.1, bf16[128,1024]{1,0:T(8,128)(2,1)} %v_hbm.1, bf16[128,1024]{1,0:T(8,128)(2,1)} %g_hbm.1, s32[64,64]{1,0:T(8,128)} %mask_hbm.1), custom_call_target="tpu_custom_call" | custom-call | tf_op jit(solution)/shard_map/pallas_call | solution.py:423
  54.1 0.9 %shard_map.77 = (bf16[128,1024]{1,0:T(8,128)(2,1)}, bf16[128,1024]{1,0:T(8,128)(2,1)}, bf16[128,1024]{1,0:T(8,128)(2,1)}) custom-call(bf16[128,1024]{1,0:T(8,128)(2,1)S(1)} %get-tuple-element.6.dq, bf16[128,1024]{1,0:T(8,128)(2,1)S(1)} %get-tuple-element.7.dk, bf16[128,1024]{1,0:T(8,128)(2,1)S(1)} %get-tuple-element.8.dv), custom_call_target="tpu_custom_call" | custom-call | tf_op jit(solution)/shard_map/pallas_call | solution.py:458

commit v6 on v5

--- a/solution.py
+++ b/solution.py
@@ -188,10 +188,9 @@
                     def _():
                         entry_copy(head, which, step).start()
 
-    def start_rest(head):
-        for which in range(2, 4):
-            for step in range(1, ulys):
-                entry_copy(head, which, step).start()
+    def start_rest(head, which):
+        for step in range(1, ulys):
+            entry_copy(head, which, step).start()
 
     def await_entry(head, which):
         entry_local(head, which).wait()
@@ -361,7 +360,7 @@
 
     for which in range(2):
         await_entry(0, which)
-    start_rest(0)
+        start_rest(0, which + 2)
 
     @pl.when(listens == 0)
     def _():
@@ -371,7 +370,7 @@
     send_band(0)
     for which in range(2):
         await_entry(1, which)
-    start_rest(1)
+        start_rest(1, which + 2)
     send_band(1)
     await_entry(0, 2)
     await_band(0, 0)

time: 55.2 us -> 55.6 us (level)
  the two profiles are of different devices: /device:TPU:56 before, /device:TPU:8 now
where the time goes in v6:
time: 55.6 us; the launch traced here: 55.4 us
  Pallas kernels  54.8 us (99%)
  between operations  0.64 us (1%)
    pallas_call x1, Pallas kernels, local(): pl.pallas_call(functools.partial(kernel, cells, ulys), out_shape=outputs,...  53.9 us

profile of v6, /device:TPU:8, one launch (start us, length us, event | category | flops | bytes accessed | tf_op | source)
XLA Modules:
  0.0 55.4 jit_solution(2815172034248561034)
XLA Ops:
  0.6 53.9 %shard_map.76 = (bf16[128,1024]{1,0:T(8,128)(2,1)S(1)}, bf16[128,1024]{1,0:T(8,128)(2,1)S(1)}, bf16[128,1024]{1,0:T(8,128)(2,1)S(1)}) custom-call(bf16[128,1024]{1,0:T(8,128)(2,1)} %q_hbm.1, bf16[128,1024]{1,0:T(8,128)(2,1)} %k_hbm.1, bf16[128,1024]{1,0:T(8,128)(2,1)} %v_hbm.1, bf16[128,1024]{1,0:T(8,128)(2,1)} %g_hbm.1, s32[64,64]{1,0:T(8,128)} %mask_hbm.1), custom_call_target="tpu_custom_call" | custom-call | tf_op jit(solution)/shard_map/pallas_call | solution.py:422
  54.5 0.9 %shard_map.77 = (bf16[128,1024]{1,0:T(8,128)(2,1)}, bf16[128,1024]{1,0:T(8,128)(2,1)}, bf16[128,1024]{1,0:T(8,128)(2,1)}) custom-call(bf16[128,1024]{1,0:T(8,128)(2,1)S(1)} %get-tuple-element.6.dq, bf16[128,1024]{1,0:T(8,128)(2,1)S(1)} %get-tuple-element.7.dk, bf16[128,1024]{1,0:T(8,128)(2,1)S(1)} %get-tuple-element.8.dv), custom_call_target="tpu_custom_call" | custom-call | tf_op jit(solution)/shard_map/pallas_call | solution.py:457
